TPU v7x, 256 devices: a whole 4x4x8 slice. The times are simulated.
256 devices in a mesh: seq: 32 (over x, z), mp: 8 (over y, core).
Axes of the slice: x: 4, y: 4, z: 8, core: 2. Of those that a mesh axis runs over, the one named last changes fastest.
Arguments:
- hidden_in: bfloat16 [64, 2048], P('mp'), may hold values from -24 to 24
- query_weight: bfloat16 [2048, 3072], P(None, 'seq'), may hold values from -0.25 to 0.25
- key_absorb: bfloat16 [16, 128, 512], replicated, may hold values from -0.5 to 0.5
- value_up: bfloat16 [16, 512, 128], replicated, may hold values from -0.25 to 0.25
- out_weight: bfloat16 [2048, 2048], P(None, 'seq'), may hold values from -0.5 to 0.5
- latent_cache: bfloat16 [64, 4096, 576], P('mp', 'seq'), may hold values from -41 to 41
- cache_lengths: int32 [64], P('mp'), may hold values from 128 to 4096, as said below
- keep_lists: int32 [64, 32, 64], P('mp', 'seq'), may hold values from 0 to 127, as said below
- drop_weights: int32 [64, 4096], P('mp', 'seq'), may hold values from 1 to 8
- pack_dest: int32 [64, 32], P('mp'), may hold values from -1 to 127, as said below
- final_gain: bfloat16 [2048], replicated, may hold values from 0.5 to 1.5
- head_weight: bfloat16 [2048, 102400], P(None, ('seq', 'mp')), may hold values from -0.125 to 0.125
- tenant_ranges: int32 [4, 2], replicated, may hold values from 0 to 102400, as said below
- tenant_ids: int32 [64], replicated, may hold values from 0 to 3
Outputs:
- packed_rows: bfloat16 [1024, 64, 576], P(('seq', 'mp'))
- packed_summary: bfloat16 [1024, 576], P(('seq', 'mp'))
- hidden_out: bfloat16 [64, 2048], P('mp', 'seq')
- state_norm: float32 [64], P('mp')
- top_logit: float32 [64], P('mp')
Inputs may be any that keep to these rules, and one draw needn't show every extreme that they name: `cache_lengths`: every length is a whole number of 128-position blocks, at least one block. Within each group of 8 requests (one index of mp) the lengths add up to 16384, and some request of the group has the full 4096. `keep_lists`: the 64 positions of a block are distinct and ascending. pack_dest[r, b] is -1 exactly when block b of request r is not live; otherwise it is owner * 4 + slot with an owner in 0 to 32 - 1 (an index of seq) and a slot in 0 to 3. Within one group of 8 requests the live blocks take every destination exactly once. Of the live blocks of one block index in one group, at most 1 go to any one owner, and those that share an owner take consecutive slots. Block index 0 is live for every request of a group, and some owner receives 1 of them. `tenant_ranges`: row t is tenant t's window [low, high) of vocabulary entries; each window holds at least 51200 entries.
All inputs are finite; a program needn't handle non-finite values.
Results may differ from a plain program's by a relative error of at most 0.0075.
Values may be sent and summed in bfloat16 or wider, within the bound.
No kernel may reach another device: no remote copies, remote signals or barrier semaphores. Data moves between devices by JAX's collectives and lax.ppermute only.
A program may use at most 128 MiB of HBM per device.

v0:
```python
import jax
import jax.numpy as jnp
from jax import lax
from jax.sharding import PartitionSpec as P

H = 16
NOPE = 128
ROPE = 64
LAT = 512
VH = 128
BLK = 128
KB = 64
TENANTS = 4
RQ = 8
NEGATIVE = -1e30
HIGHEST = lax.Precision.HIGHEST


def merged(x, axis, combine):
    everything = jax.tree.map(lambda part: lax.all_gather(part, axis), x)
    initial = jax.tree.map(lambda part: part[0], everything)

    def step(k, so_far):
        return combine(so_far, jax.tree.map(lambda part: part[k], everything))

    return lax.fori_loop(1, lax.axis_size(axis), step, initial)


def compact_blocks(block_rows, keep_onehot, weights_dropped):
    kept_rows = jnp.einsum(
        "nkt,ntc->nkc", keep_onehot, block_rows, preferred_element_type=jnp.float32
    ).astype(jnp.bfloat16)
    weight_mass = jnp.sum(weights_dropped.astype(jnp.float32), axis=1)
    summed = jnp.einsum(
        "nt,ntc->nc", weights_dropped, block_rows, preferred_element_type=jnp.float32
    )
    summary = (summed / weight_mass[:, None]).astype(jnp.bfloat16)
    return (kept_rows, summary)


def attend_blocks(query_lat, query_rope, kept_rows, summary, usable):
    score_scale = (NOPE + ROPE) ** (-0.5)
    row_scores = (
        jnp.einsum(
            "nhl,nkl->nhk", query_lat, kept_rows[:, :, :LAT], preferred_element_type=jnp.float32
        )
        + jnp.einsum(
            "nhr,nkr->nhk", query_rope, kept_rows[:, :, LAT:], preferred_element_type=jnp.float32
        )
    ) * score_scale
    summ_scores = (
        jnp.einsum("nhl,nl->nh", query_lat, summary[:, :LAT], preferred_element_type=jnp.float32)
        + jnp.einsum("nhr,nr->nh", query_rope, summary[:, LAT:], preferred_element_type=jnp.float32)
    ) * score_scale
    summ_scores = summ_scores + jnp.log(jnp.float32(BLK - KB))
    row_scores = jnp.where(usable[:, None, None], row_scores, NEGATIVE)
    summ_scores = jnp.where(usable[:, None], summ_scores, NEGATIVE)
    maxima = jnp.maximum(jnp.max(row_scores, axis=2), summ_scores)
    row_weights = jnp.where(usable[:, None, None], jnp.exp(row_scores - maxima[:, :, None]), 0.0)
    summ_weights = jnp.where(usable[:, None], jnp.exp(summ_scores - maxima), 0.0)
    totals = jnp.sum(row_weights, axis=2) + summ_weights
    weighted = jnp.einsum(
        "nhk,nkl->nhl", row_weights, kept_rows[:, :, :LAT].astype(jnp.float32), precision=HIGHEST
    )
    weighted = weighted + summ_weights[:, :, None] * summary[:, None, :LAT].astype(jnp.float32)
    return (maxima, totals, weighted)


def per_request(maxima, totals, weighted, owner_of):
    request_max = jnp.max(jnp.where(owner_of[:, :, None], maxima[None, :, :], NEGATIVE), axis=1)
    shifted = jnp.where(owner_of[:, :, None], maxima[None, :, :] - request_max[:, None, :], 0.0)
    factor = jnp.where(owner_of[:, :, None], jnp.exp(shifted), 0.0)
    request_total = jnp.einsum("rnh,nh->rh", factor, totals, precision=HIGHEST)
    request_sum = jnp.einsum("rnh,nhl->rhl", factor, weighted, precision=HIGHEST)
    return (request_max, request_total, request_sum)


def combine_partial(former, latter):
    former_max, former_total, former_sum = former
    latter_max, latter_total, latter_sum = latter
    joined = jnp.maximum(former_max, latter_max)
    former_factor = jnp.exp(former_max - joined)
    latter_factor = jnp.exp(latter_max - joined)
    return (
        joined,
        former_factor * former_total + latter_factor * latter_total,
        former_factor[:, :, None] * former_sum + latter_factor[:, :, None] * latter_sum,
    )


def body(
    hidden_in,
    query_weight,
    key_absorb,
    value_up,
    out_weight,
    latent_cache,
    cache_lengths,
    keep_lists,
    drop_weights,
    pack_dest,
    final_gain,
    head_weight,
    tenant_ranges,
    tenant_ids,
):
    seq_count = lax.axis_size("seq")
    mp_count = lax.axis_size("mp")
    seq_index = lax.axis_index("seq")
    mp_index = lax.axis_index("mp")
    capacity = max(1, RQ // seq_count)
    slot_count = RQ // 2
    row_width = LAT + ROPE
    query_part = jnp.dot(hidden_in, query_weight, preferred_element_type=jnp.float32).astype(
        jnp.bfloat16
    )
    query_full = lax.all_gather(query_part, "seq", axis=1, tiled=True).reshape(RQ, H, NOPE + ROPE)
    query_lat = jnp.einsum(
        "rhn,hnl->rhl", query_full[:, :, :NOPE], key_absorb, preferred_element_type=jnp.float32
    ).astype(jnp.bfloat16)
    query_rope = query_full[:, :, NOPE:]
    positions = jnp.arange(BLK, dtype=jnp.int32)
    keep_onehot = keep_lists[:, 0, :, None] == positions[None, None, :]
    kept_flag = jnp.sum(keep_onehot.astype(jnp.int32), axis=1)
    weights_dropped = (drop_weights * (1 - kept_flag)).astype(jnp.bfloat16)
    live_here = cache_lengths > seq_index * BLK
    dest_here = lax.dynamic_slice_in_dim(pack_dest, seq_index, 1, 1)[:, 0]
    send_slot = dest_here // slot_count * capacity + dest_here % slot_count % capacity
    slot_range = jnp.arange(seq_count * capacity, dtype=jnp.int32)
    send_onehot = ((send_slot[None, :] == slot_range[:, None]) & live_here[None, :]).astype(
        jnp.bfloat16
    )
    targets = seq_index * slot_count + jnp.arange(slot_count, dtype=jnp.int32)
    slot_match = (pack_dest[None, :, :] == targets[:, None, None]).astype(jnp.int32)
    block_range = jnp.arange(pack_dest.shape[1], dtype=jnp.int32)
    source_of = jnp.sum(slot_match * block_range[None, None, :], axis=(1, 2))
    request_of = jnp.sum(slot_match, axis=2)
    request_index = jnp.sum(request_of * jnp.arange(RQ, dtype=jnp.int32)[None, :], axis=1)
    pick_index = source_of * capacity + jnp.arange(slot_count, dtype=jnp.int32) % capacity
    owner_of = jnp.transpose(request_of) > 0
    local_rows, local_summary = compact_blocks(
        latent_cache, keep_onehot.astype(jnp.bfloat16), weights_dropped
    )
    send_rows = jnp.einsum(
        "jr,rkc->jkc", send_onehot, local_rows, preferred_element_type=jnp.float32
    )
    send_rows = send_rows.astype(jnp.bfloat16).reshape(seq_count, capacity, KB, row_width)
    send_summary = jnp.dot(send_onehot, local_summary, preferred_element_type=jnp.float32)
    send_summary = send_summary.astype(jnp.bfloat16).reshape(seq_count, capacity, row_width)
    recv_rows, recv_summary = (
        lax.all_to_all(send_rows, "seq", split_axis=0, concat_axis=0, tiled=True),
        lax.all_to_all(send_summary, "seq", split_axis=0, concat_axis=0, tiled=True),
    )
    packed_rows = jnp.take(
        recv_rows.reshape(seq_count * capacity, KB, row_width), pick_index, axis=0
    )
    packed_summary = jnp.take(
        recv_summary.reshape(seq_count * capacity, row_width), pick_index, axis=0
    )
    slot_query_lat = jnp.take(query_lat, request_index, axis=0)
    slot_query_rope = jnp.take(query_rope, request_index, axis=0)
    usable = jnp.ones((slot_count,), dtype=bool)
    maxima, totals, weighted = attend_blocks(
        slot_query_lat, slot_query_rope, packed_rows, packed_summary, usable
    )
    partial_value = per_request(maxima, totals, weighted, owner_of)
    request_max, request_total, request_sum = merged(partial_value, "seq", combine_partial)
    attended = (request_sum / request_total[:, :, None]).astype(jnp.bfloat16)
    values = jnp.einsum("rhl,hlv->rhv", attended, value_up, preferred_element_type=jnp.float32)
    values = values.astype(jnp.bfloat16).reshape(RQ, H * VH)
    col_width = out_weight.shape[1]
    residual = lax.dynamic_slice_in_dim(hidden_in, seq_index * col_width, col_width, 1)
    hidden_out = (
        residual.astype(jnp.float32)
        + jnp.dot(values, out_weight, preferred_element_type=jnp.float32)
    ).astype(jnp.bfloat16)
    gathered = lax.all_gather(hidden_out[None], ("seq", "mp"), axis=0, tiled=True)
    all_rows = gathered.reshape(seq_count, mp_count, RQ, col_width).transpose(1, 2, 0, 3)
    all_rows = all_rows.reshape(mp_count * RQ, seq_count * col_width)
    rows_f = all_rows.astype(jnp.float32)
    mean_sq = jnp.mean(rows_f * rows_f, axis=1)
    norms_all = jnp.sqrt(mean_sq)
    normed = (
        rows_f * lax.rsqrt(mean_sq + 1e-06)[:, None] * final_gain.astype(jnp.float32)[None, :]
    ).astype(jnp.bfloat16)
    logits = jnp.dot(normed, head_weight, preferred_element_type=jnp.float32)
    vocab_width = head_weight.shape[1]
    device_index = seq_index * mp_count + mp_index
    columns = device_index * vocab_width + jnp.arange(vocab_width, dtype=jnp.int32)
    tenant_onehot = (tenant_ids[:, None] == jnp.arange(TENANTS, dtype=jnp.int32)[None, :]).astype(
        jnp.int32
    )
    window_low = jnp.sum(tenant_onehot * tenant_ranges[None, :, 0], axis=1)
    window_high = jnp.sum(tenant_onehot * tenant_ranges[None, :, 1], axis=1)
    allowed = (columns[None, :] >= window_low[:, None]) & (columns[None, :] < window_high[:, None])
    local_best = jnp.max(jnp.where(allowed, logits, NEGATIVE), axis=1)
    best_all = lax.pmax(local_best, ("seq", "mp"))
    row_start = mp_index * RQ
    state_norm = lax.dynamic_slice_in_dim(norms_all, row_start, RQ, 0)
    top_logit = lax.dynamic_slice_in_dim(best_all, row_start, RQ, 0)
    return (packed_rows, packed_summary, hidden_out, state_norm, top_logit)


def solution(mesh):
    in_specs = (
        P("mp", None),
        P(None, "seq"),
        P(),
        P(),
        P(None, "seq"),
        P("mp", "seq", None),
        P("mp"),
        P("mp", "seq", None),
        P("mp", "seq"),
        P("mp", None),
        P(),
        P(None, ("seq", "mp")),
        P(),
        P(),
    )
    out_specs = (
        P(("seq", "mp"), None, None),
        P(("seq", "mp"), None),
        P("mp", "seq"),
        P("mp"),
        P("mp"),
    )
    return jax.shard_map(body, mesh=mesh, in_specs=in_specs, out_specs=out_specs, check_vma=False)
```

profile of v0, /device:TPU:1, one launch (start us, length us, event | category | flops | bytes accessed | tf_op | source)
XLA Modules:
  0.0 443.5 jit_solution(3956830009259574971)
XLA Ops:
  7.2 1.0 dynamic-slice_reduce_fusion
  10.5 1.7 fusion.37
  14.5 11.9 %all-to-all-start.1 = ((bf16[32,2,288]{2,1,0:T(2,128)(2,1)}), bf16[32,2,288]{2,1,0:T(2,128)(2,1)S(1)}, u32[]{:S(2)}, u32[]{:S(2)}) async-start(bf16[32,2,288]{2,1,0:T(2,128)(2,1)} %reshape.212), calls=%async_computation.1 | async-start | bytes 98304 | tf_op jit(solution)/shard_map/all_to_all | solution.py:152
  26.3 1.2 convolution_convert_fusion
  28.6 2.4 copy.83
  31.0 4.1 all-to-all-done.1
  35.1 5.3 %all-to-all-start = ((bf16[32,1,64,576]{3,2,1,0:T(8,128)(2,1)}), bf16[32,1,64,576]{3,2,1,0:T(8,128)(2,1)}, u32[]{:S(2)}, u32[]{:S(2)}) async-start(bf16[32,1,64,576]{3,2,1,0:T(8,128)(2,1)} %copy.83), calls=%async_computation | async-start | bytes 5242880 | tf_op jit(solution)/shard_map/all_to_all | solution.py:151
  40.8 88.3 %all-gather.4 = bf16[32,96,8]{1,2,0:T(8,128)(2,1)S(1)} all-gather(bf16[1,96,8]{1,2,0:T(8,128)(2,1)S(1)} %fusion.10), channel_id=1, replica_groups=mesh['seq'=32,'mp'=8] {'seq'}, dimensions={0}, use_global_device_ids=true | all-gather | bytes 50688 | tf_op jit(solution)/shard_map/all_gather | solution.py:117
  132.6 2.4 gather_fusion
  136.4 1.2 convolution_bitcast_fusion
  137.8 33.3 %all-gather = f32[256,16]{1,0:T(8,128)S(1)} all-gather(f32[8,16]{1,0:T(8,128)S(1)} %copy.89), channel_id=2, replica_groups=mesh['seq'=32,'mp'=8] {'seq'}, dimensions={0}, use_global_device_ids=true | all-gather | bytes 16896 | tf_op jit(solution)/shard_map/all_gather | solution.py:20
  171.4 33.9 %all-gather.1 = f32[256,16]{1,0:T(8,128)S(1)} all-gather(f32[8,16]{1,0:T(8,128)S(1)} %bitcast.111), channel_id=3, replica_groups=mesh['seq'=32,'mp'=8] {'seq'}, dimensions={0}, use_global_device_ids=true | all-gather | bytes 16896 | tf_op jit(solution)/shard_map/all_gather | solution.py:20
  205.4 41.6 %all-gather.7.cloned.1.call-done = f32[256,16,512]{2,0,1:T(8,128)} async-done(((f32[8,16,512]{2,0,1:T(8,128)}), f32[256,16,512]{2,0,1:T(8,128)}) %all-gather.7.cloned.1.call-update) | async-done | bytes 8388624 | tf_op jit(solution)/shard_map/all_gather | solution.py:20
  248.1 38.1 %while.19 = (s32[]{:T(128)}, f32[8,16]{1,0:T(8,128)S(1)}, f32[8,16]{1,0:T(8,128)S(1)}, f32[8,16,512]{2,1,0:T(8,128)S(1)}, f32[32,8,16]{2,1,0:T(8,128)S(1)}, /*in...) while((s32[]{:T(128)}, f32[8,16]{1,0:T(8,128)S(1)}, ...), condition=%wide.region_9.10_spmd, body=%wide.region_8.9_spmd.sunk | while | flops 197381 | bytes 1315991 | solution.py:26
  248.1 1.0 constant_dynamic-slice_fusion.2
  255.5 1.0 constant_dynamic-slice_fusion.2
  261.7 1.0 constant_dynamic-slice_fusion.2
  270.3 1.0 constant_dynamic-slice_fusion.2
  286.3 2.1 fusion.9
  288.4 67.2 %all-gather.3 = bf16[2048,64]{1,0:T(8,128)(2,1)S(1)} all-gather(bf16[8,64]{1,0:T(8,128)(2,1)S(1)} %fusion.9), channel_id=5, replica_groups=mesh['seq'=32,'mp'=8] {'seq','mp'}, dimensions={0}, use_global_device_ids=true | all-gather | bytes 263168 | tf_op jit(solution)/shard_map/all_gather | solution.py:177
  356.2 1.3 copy.135
  357.5 1.6 reshape.150
  359.2 2.2 fusion.5
  361.3 74.2 %pmax.7 = f32[64]{0:T(128)S(1)} all-reduce(f32[64]{0:T(128)S(1)} %fusion.5), channel_id=1, replica_groups=mesh['seq'=32,'mp'=8] {'seq','mp'}, use_global_device_ids=true, to_apply=%region_15.16 | all-reduce | flops 64 | bytes 512 | tf_op jit(solution)/shard_map/pmax | solution.py:197
  (182 shorter events, 47.3 us)
Async XLA Ops:
  7.2 122.2 %copy-start = (bf16[16,128,512]{2,1,0:T(8,128)(2,1)S(1)}, bf16[16,128,512]{2,1,0:T(8,128)(2,1)}, u32[]{:S(2)}) copy-start(bf16[16,128,512]{2,1,0:T(8,128)(2,1)} %param.18) | copy-start | bytes 6291460
  7.2 19.2 %copy-start.1 = (bf16[8,128,576]{1,2,0:T(8,128)(2,1)S(1)}, bf16[8,128,576]{1,2,0:T(8,128)(2,1)}, u32[]{:S(2)}) copy-start(bf16[8,128,576]{1,2,0:T(8,128)(2,1)} %param.21) | copy-start | bytes 3538948
  14.5 20.7 %all-to-all-start.1 = ((bf16[32,2,288]{2,1,0:T(2,128)(2,1)}), bf16[32,2,288]{2,1,0:T(2,128)(2,1)S(1)}, u32[]{:S(2)}, u32[]{:S(2)}) async-start(bf16[32,2,288]{2,1,0:T(2,128)(2,1)} %reshape.212), calls=%async_computation.1 | async-start | bytes 98304 | tf_op jit(solution)/shard_map/all_to_all | solution.py:152
  31.0 9.5 %copy-start.3 = (bf16[2048,96]{0,1:T(8,128)(2,1)S(1)}, bf16[2048,96]{0,1:T(8,128)(2,1)}, u32[]{:S(2)}) copy-start(bf16[2048,96]{0,1:T(8,128)(2,1)} %param.17) | copy-start | bytes 1179652
  31.0 9.6 %copy-start.5 = (bf16[8,2048]{1,0:T(8,128)(2,1)S(1)}, bf16[8,2048]{1,0:T(8,128)(2,1)}, u32[]{:S(2)}) copy-start(bf16[8,2048]{1,0:T(8,128)(2,1)} %param.16) | copy-start | bytes 98308
  35.1 97.5 %all-to-all-start = ((bf16[32,1,64,576]{3,2,1,0:T(8,128)(2,1)}), bf16[32,1,64,576]{3,2,1,0:T(8,128)(2,1)}, u32[]{:S(2)}, u32[]{:S(2)}) async-start(bf16[32,1,64,576]{3,2,1,0:T(8,128)(2,1)} %copy.83), calls=%async_computation | async-start | bytes 5242880 | tf_op jit(solution)/shard_map/all_to_all | solution.py:151
  40.5 89.3 %copy-start.7 = (s32[8,32]{1,0:T(8,128)S(1)}, s32[8,32]{1,0:T(8,128)}, u32[]{:S(2)}) copy-start(s32[8,32]{1,0:T(8,128)} %param.25) | copy-start | bytes 3076
  40.5 206.4 %all-gather.7.cloned.1.call-start = ((), (), s32[]{:S(2)}) async-start(), calls=%async_computation.2 | async-start | bytes 8650752 | tf_op jit(solution)/shard_map/all_gather | solution.py:20
  129.7 7.9 %copy-start.9 = (bf16[2048]{0:T(1024)(128)(2,1)S(1)}, bf16[2048]{0:T(1024)(128)(2,1)}, u32[]{:S(2)}) copy-start(bf16[2048]{0:T(1024)(128)(2,1)} %param.26) | copy-start | bytes 12292
  129.7 7.9 %copy-start.10 = (s32[4,2]{0,1:T(2,128)S(1)}, s32[4,2]{0,1:T(2,128)}, u32[]{:S(2)}) copy-start(s32[4,2]{0,1:T(2,128)} %param.28) | copy-start | bytes 100
  129.7 7.9 %copy-start.11 = (s32[64]{0:T(128)S(1)}, s32[64]{0:T(128)}, u32[]{:S(2)}) copy-start(s32[64]{0:T(128)} %param.29) | copy-start | bytes 772
  132.2 115.7 %copy-start.6 = (bf16[4,576]{1,0:T(4,128)(2,1)}, bf16[4,576]{1,0:T(4,128)(2,1)S(1)}, u32[]{:S(2)}) copy-start(bf16[4,576]{1,0:T(4,128)(2,1)S(1)} %broadcast_select_fusion.7) | copy-start | bytes 13828
  135.1 113.0 %copy-start.2 = (bf16[4,64,576]{2,1,0:T(8,128)(2,1)}, bf16[4,64,576]{2,1,0:T(8,128)(2,1)S(1)}, u32[]{:S(2)}) copy-start(bf16[4,64,576]{2,1,0:T(8,128)(2,1)S(1)} %broadcast_select_fusion) | copy-start | bytes 884740
  248.1 38.2 %copy-start.4 = (bf16[2048,64]{0,1:T(8,128)(2,1)S(1)}, bf16[2048,64]{0,1:T(8,128)(2,1)}, u32[]{:S(2)}) copy-start(bf16[2048,64]{0,1:T(8,128)(2,1)} %param.20) | copy-start | bytes 786436
  288.4 70.7 %copy-start.8 = (bf16[8,64]{1,0:T(8,128)(2,1)}, bf16[8,64]{1,0:T(8,128)(2,1)S(1)}, u32[]{:S(2)}) copy-start(bf16[8,64]{1,0:T(8,128)(2,1)S(1)} %fusion.9) | copy-start | bytes 3076
Sparse Core Ops, SparseCore 0:
  137.7 109.1 all-gather.6
where the time goes:
time: 445 us; the launch traced here: 444 us
  blocking collectives  297 us (67%)
  waiting for transfers between devices  45.7 us (10%)
  local copies, waits for them, and re-layouts  45.3 us (10%)
  starting transfers between devices  17.2 us (4%)
  between operations  14.5 us (3%)
  other arithmetic  11.5 us (3%)
  matrix products  11.5 us (3%)
    all_gather x1, blocking collectives, body(): lax.all_gather(query_part, 'seq', axis=1, tiled=True)  88.3 us
    pmax x1, blocking collectives, body(): best_all = lax.pmax(local_best, ('seq', 'mp'))  74.2 us
    all_gather x2, blocking collectives, merged(): everything = jax.tree.map(lambda part: lax.all_gather(part, axis), x)  67.2 us
    all_gather x1, blocking collectives, body(): lax.all_gather(hidden_out[None], ('seq', 'mp'), axis=0, tiled=True)  67.2 us
    all_gather x1, waiting for transfers between devices, merged(): everything = jax.tree.map(lambda part: lax.all_gather(part, axis), x)  41.6 us
    dynamic_slice x31, local copies, waits for them, and re-layouts, step(): return combine(so_far, jax.tree.map(lambda part: part[k], everything))  30.3 us
    all_to_all x1, starting transfers between devices, body(): lax.all_to_all(send_summary, 'seq', split_axis=0, concat_axis=0, tiled=True)  11.9 us
  transfers between devices with their start and end apart: 3, of which 2 were waited for; matrix products, arithmetic and copies ran while one was open for 2% of the time, Pallas kernels for 0%

commit v1 on v0

--- a/solution.py
+++ b/solution.py
@@ -174,7 +174,12 @@
         residual.astype(jnp.float32)
         + jnp.dot(values, out_weight, preferred_element_type=jnp.float32)
     ).astype(jnp.bfloat16)
-    gathered = lax.all_gather(hidden_out[None], ("seq", "mp"), axis=0, tiled=True)
+    gathered = jnp.concatenate(
+        lax.all_to_all(
+            jnp.stack([hidden_out[None]] * lax.axis_size(("seq", "mp"))), ("seq", "mp"), 0, 0
+        ),
+        axis=0,
+    )
     all_rows = gathered.reshape(seq_count, mp_count, RQ, col_width).transpose(1, 2, 0, 3)
     all_rows = all_rows.reshape(mp_count * RQ, seq_count * col_width)
     rows_f = all_rows.astype(jnp.float32)

time: 445 us -> 404 us (0.908)
  blocking collectives: 297 us -> 228 us
  waiting for transfers between devices: 45.7 us -> 61.4 us
  starting transfers between devices: 17.2 us -> 26.5 us
    all_gather x1 -> x0, blocking collectives: 67.2 us -> none  [body(): lax.all_gather(hidden_out[None], ('seq', 'mp'), axis=0, tiled=True)]
    all_to_all x0 -> x1, waiting for transfers between devices: none -> 15.3 us  [body(): lax.all_to_all(jnp.stack([hidden_out[None]] * lax.axis_size(('seq', 'mp')...]
    all_to_all x0 -> x1, starting transfers between devices: none -> 9.24 us  [body(): lax.all_to_all(jnp.stack([hidden_out[None]] * lax.axis_size(('seq', 'mp')...]
  transfers between devices with their start and end apart: 3 -> 4, of which waited for: 2 -> 3; matrix products, arithmetic and copies ran while one was open for 2% -> 2% of each run, Pallas kernels for 0% -> 0%
where the time goes in v1:
time: 404 us; the launch traced here: 402 us
  blocking collectives  228 us (56%)
  waiting for transfers between devices  61.4 us (15%)
  local copies, waits for them, and re-layouts  46.8 us (12%)
  starting transfers between devices  26.5 us (7%)
  between operations  14.5 us (4%)
  other arithmetic  12.6 us (3%)
  matrix products  11.6 us (3%)
    all_gather x1, blocking collectives, body(): lax.all_gather(query_part, 'seq', axis=1, tiled=True)  88.3 us
    pmax x1, blocking collectives, body(): best_all = lax.pmax(local_best, ('seq', 'mp'))  72.6 us
    all_gather x2, blocking collectives, merged(): everything = jax.tree.map(lambda part: lax.all_gather(part, axis), x)  67.1 us
    all_gather x1, waiting for transfers between devices, merged(): everything = jax.tree.map(lambda part: lax.all_gather(part, axis), x)  41.9 us
    dynamic_slice x31, local copies, waits for them, and re-layouts, step(): return combine(so_far, jax.tree.map(lambda part: part[k], everything))  30.3 us
    all_to_all x1, waiting for transfers between devices, body(): lax.all_to_all(jnp.stack([hidden_out[None]] * lax.axis_size(('seq', 'mp')...  15.3 us
    all_to_all x1, starting transfers between devices, body(): lax.all_to_all(send_summary, 'seq', split_axis=0, concat_axis=0, tiled=True)  11.9 us
    all_to_all x1, starting transfers between devices, body(): lax.all_to_all(jnp.stack([hidden_out[None]] * lax.axis_size(('seq', 'mp')...  9.24 us
  transfers between devices with their start and end apart: 4, of which 3 were waited for; matrix products, arithmetic and copies ran while one was open for 2% of the time, Pallas kernels for 0%

profile of v1, /device:TPU:1, one launch (start us, length us, event | category | flops | bytes accessed | tf_op | source)
XLA Modules:
  0.0 402.2 jit_solution(15729309356285953773)
XLA Ops:
  7.2 1.0 dynamic-slice_reduce_fusion
  10.5 1.7 fusion.37
  14.5 11.9 %all-to-all-start.1 = ((bf16[32,2,288]{2,1,0:T(2,128)(2,1)}), bf16[32,2,288]{2,1,0:T(2,128)(2,1)S(1)}, u32[]{:S(2)}, u32[]{:S(2)}) async-start(bf16[32,2,288]{2,1,0:T(2,128)(2,1)} %reshape.206), calls=%async_computation.1 | async-start | bytes 98304 | tf_op jit(solution)/shard_map/all_to_all | solution.py:152
  26.3 1.2 convolution_convert_fusion
  28.6 2.4 copy.126
  31.0 4.1 %all-to-all-done.1 = bf16[32,2,288]{2,1,0:T(2,128)(2,1)S(1)} async-done(((bf16[32,2,288]{2,1,0:T(2,128)(2,1)}), bf16[32,2,288]{2,1,0:T(2,128)(2,1)S(1)}, u32[]{:S(2)}, u32[]{:S(2)}) %all-to-all-start.1) | async-done | bytes 36896 | tf_op jit(solution)/shard_map/all_to_all | solution.py:152
  35.1 5.3 %all-to-all-start = ((bf16[32,1,64,576]{3,2,1,0:T(8,128)(2,1)}), bf16[32,1,64,576]{3,2,1,0:T(8,128)(2,1)}, u32[]{:S(2)}, u32[]{:S(2)}) async-start(bf16[32,1,64,576]{3,2,1,0:T(8,128)(2,1)} %copy.126), calls=%async_computation | async-start | bytes 5242880 | tf_op jit(solution)/shard_map/all_to_all | solution.py:151
  40.8 88.3 %all-gather.3 = bf16[32,96,8]{1,2,0:T(8,128)(2,1)S(1)} all-gather(bf16[1,96,8]{1,2,0:T(8,128)(2,1)S(1)} %fusion.10), channel_id=1, replica_groups=mesh['seq'=32,'mp'=8] {'seq'}, dimensions={0}, use_global_device_ids=true | all-gather | bytes 50688 | tf_op jit(solution)/shard_map/all_gather | solution.py:117
  132.6 2.4 gather_fusion
  136.4 1.2 convolution_bitcast_fusion
  137.7 32.5 %all-gather = f32[256,16]{1,0:T(8,128)S(1)} all-gather(f32[8,16]{1,0:T(8,128)S(1)} %copy.132), channel_id=2, replica_groups=mesh['seq'=32,'mp'=8] {'seq'}, dimensions={0}, use_global_device_ids=true | all-gather | bytes 16896 | tf_op jit(solution)/shard_map/all_gather | solution.py:20
  170.5 34.6 %all-gather.1 = f32[256,16]{1,0:T(8,128)S(1)} all-gather(f32[8,16]{1,0:T(8,128)S(1)} %bitcast.114), channel_id=3, replica_groups=mesh['seq'=32,'mp'=8] {'seq'}, dimensions={0}, use_global_device_ids=true | all-gather | bytes 16896 | tf_op jit(solution)/shard_map/all_gather | solution.py:20
  205.0 41.9 %all-gather.6.cloned.1.call-done = f32[256,16,512]{2,0,1:T(8,128)} async-done(((f32[8,16,512]{2,0,1:T(8,128)}), f32[256,16,512]{2,0,1:T(8,128)}) %all-gather.6.cloned.1.call-update) | async-done | bytes 8388624 | tf_op jit(solution)/shard_map/all_gather | solution.py:20
  248.1 38.1 %while.19 = (s32[]{:T(128)}, f32[8,16]{1,0:T(8,128)S(1)}, f32[8,16]{1,0:T(8,128)S(1)}, f32[8,16,512]{2,1,0:T(8,128)S(1)}, f32[32,8,16]{2,1,0:T(8,128)S(1)}, /*in...) while((s32[]{:T(128)}, f32[8,16]{1,0:T(8,128)S(1)}, ...), condition=%wide.region_9.10_spmd, body=%wide.region_8.9_spmd.sunk | while | flops 197381 | bytes 1315991 | solution.py:26
  248.2 1.0 constant_dynamic-slice_fusion.2
  286.3 2.1 fusion.9
  288.6 1.0 reshape.208
  289.6 9.2 %all-to-all-start.2 = ((bf16[256,2,256]{2,1,0:T(2,128)(2,1)}), bf16[256,2,256]{2,1,0:T(2,128)(2,1)S(1)}, u32[]{:S(2)}, u32[]{:S(2)}) async-start(bf16[256,2,256]{2,1,0:T(2,128)(2,1)} %reshape.208), calls=%async_computation.2 | async-start | bytes 524288 | tf_op jit(solution)/shard_map/all_to_all | solution.py:178
  299.0 15.3 %all-to-all-done.2 = bf16[256,2,256]{2,1,0:T(2,128)(2,1)S(1)} async-done(((bf16[256,2,256]{2,1,0:T(2,128)(2,1)}), bf16[256,2,256]{2,1,0:T(2,128)(2,1)S(1)}, u32[]{:S(2)}, u32[]{:S(2)}) %all-to-all-start.2) | async-done | bytes 262176 | tf_op jit(solution)/shard_map/all_to_all | solution.py:178
  315.0 1.1 bitcast_convert_fusion
  316.2 1.8 copy.140
  318.1 1.1 reshape.151
  319.3 2.3 fusion.5
  321.6 72.6 %pmax.7 = f32[64]{0:T(128)S(1)} all-reduce(f32[64]{0:T(128)S(1)} %fusion.5), channel_id=1, replica_groups=mesh['seq'=32,'mp'=8] {'seq','mp'}, use_global_device_ids=true, to_apply=%region_15.16 | all-reduce | flops 64 | bytes 512 | tf_op jit(solution)/shard_map/pmax | solution.py:202
  (186 shorter events, 50.5 us)
Async XLA Ops:
  7.2 122.2 %copy-start = (bf16[16,128,512]{2,1,0:T(8,128)(2,1)S(1)}, bf16[16,128,512]{2,1,0:T(8,128)(2,1)}, u32[]{:S(2)}) copy-start(bf16[16,128,512]{2,1,0:T(8,128)(2,1)} %param.18) | copy-start | bytes 6291460
  7.2 19.2 %copy-start.1 = (bf16[8,128,576]{1,2,0:T(8,128)(2,1)S(1)}, bf16[8,128,576]{1,2,0:T(8,128)(2,1)}, u32[]{:S(2)}) copy-start(bf16[8,128,576]{1,2,0:T(8,128)(2,1)} %param.21) | copy-start | bytes 3538948
  14.5 20.7 %all-to-all-start.1 = ((bf16[32,2,288]{2,1,0:T(2,128)(2,1)}), bf16[32,2,288]{2,1,0:T(2,128)(2,1)S(1)}, u32[]{:S(2)}, u32[]{:S(2)}) async-start(bf16[32,2,288]{2,1,0:T(2,128)(2,1)} %reshape.206), calls=%async_computation.1 | async-start | bytes 98304 | tf_op jit(solution)/shard_map/all_to_all | solution.py:152
  31.0 9.6 %copy-start.3 = (bf16[2048,96]{0,1:T(8,128)(2,1)S(1)}, bf16[2048,96]{0,1:T(8,128)(2,1)}, u32[]{:S(2)}) copy-start(bf16[2048,96]{0,1:T(8,128)(2,1)} %param.17) | copy-start | bytes 1179652
  31.0 9.6 %copy-start.5 = (bf16[8,2048]{1,0:T(8,128)(2,1)S(1)}, bf16[8,2048]{1,0:T(8,128)(2,1)}, u32[]{:S(2)}) copy-start(bf16[8,2048]{1,0:T(8,128)(2,1)} %param.16) | copy-start | bytes 98308
  35.1 97.5 %all-to-all-start = ((bf16[32,1,64,576]{3,2,1,0:T(8,128)(2,1)}), bf16[32,1,64,576]{3,2,1,0:T(8,128)(2,1)}, u32[]{:S(2)}, u32[]{:S(2)}) async-start(bf16[32,1,64,576]{3,2,1,0:T(8,128)(2,1)} %copy.126), calls=%async_computation | async-start | bytes 5242880 | tf_op jit(solution)/shard_map/all_to_all | solution.py:151
  40.5 89.3 %copy-start.7 = (s32[8,32]{1,0:T(8,128)S(1)}, s32[8,32]{1,0:T(8,128)}, u32[]{:S(2)}) copy-start(s32[8,32]{1,0:T(8,128)} %param.25) | copy-start | bytes 3076
  40.5 206.4 %all-gather.6.cloned.1.call-start = ((), (), s32[]{:S(2)}) async-start(), calls=%async_computation.3 | async-start | bytes 8650752 | tf_op jit(solution)/shard_map/all_gather | solution.py:20
  132.2 115.9 %copy-start.6 = (bf16[4,576]{1,0:T(4,128)(2,1)}, bf16[4,576]{1,0:T(4,128)(2,1)S(1)}, u32[]{:S(2)}) copy-start(bf16[4,576]{1,0:T(4,128)(2,1)S(1)} %broadcast_select_fusion.7) | copy-start | bytes 13828
  135.1 113.0 %copy-start.2 = (bf16[4,64,576]{2,1,0:T(8,128)(2,1)}, bf16[4,64,576]{2,1,0:T(8,128)(2,1)S(1)}, u32[]{:S(2)}) copy-start(bf16[4,64,576]{2,1,0:T(8,128)(2,1)S(1)} %broadcast_select_fusion) | copy-start | bytes 884740
  248.1 38.2 %copy-start.4 = (bf16[2048,64]{0,1:T(8,128)(2,1)S(1)}, bf16[2048,64]{0,1:T(8,128)(2,1)}, u32[]{:S(2)}) copy-start(bf16[2048,64]{0,1:T(8,128)(2,1)} %param.20) | copy-start | bytes 786436
  286.3 12.6 %copy-start.9 = (bf16[2048]{0:T(1024)(128)(2,1)S(1)}, bf16[2048]{0:T(1024)(128)(2,1)}, u32[]{:S(2)}) copy-start(bf16[2048]{0:T(1024)(128)(2,1)} %param.26) | copy-start | bytes 12292
  286.3 12.6 %copy-start.10 = (s32[4,2]{0,1:T(2,128)S(1)}, s32[4,2]{0,1:T(2,128)}, u32[]{:S(2)}) copy-start(s32[4,2]{0,1:T(2,128)} %param.28) | copy-start | bytes 100
  286.3 12.6 %copy-start.11 = (s32[64]{0:T(128)S(1)}, s32[64]{0:T(128)}, u32[]{:S(2)}) copy-start(s32[64]{0:T(128)} %param.29) | copy-start | bytes 772
  288.5 27.6 %copy-start.8 = (bf16[8,64]{1,0:T(8,128)(2,1)}, bf16[8,64]{1,0:T(8,128)(2,1)S(1)}, u32[]{:S(2)}) copy-start(bf16[8,64]{1,0:T(8,128)(2,1)S(1)} %fusion.9) | copy-start | bytes 3076
  289.6 24.7 %all-to-all-start.2 = ((bf16[256,2,256]{2,1,0:T(2,128)(2,1)}), bf16[256,2,256]{2,1,0:T(2,128)(2,1)S(1)}, u32[]{:S(2)}, u32[]{:S(2)}) async-start(bf16[256,2,256]{2,1,0:T(2,128)(2,1)} %reshape.208), calls=%async_computation.2 | async-start | bytes 524288 | tf_op jit(solution)/shard_map/all_to_all | solution.py:178
Sparse Core Ops, SparseCore 0:
  137.7 109.1 all-gather.5
